TPU v7x, 32 devices: a whole 2x2x4 slice. The times are simulated.
32 devices in a mesh: dp: 8 (over z, x), tensor: 4 (over y, core).
Axes of the slice: x: 2, y: 2, z: 4, core: 2. Of those that a mesh axis runs over, the one named last changes fastest.
Arguments:
- source_rows: bfloat16 [2, 2048, 3072], P(None, ('dp', 'tensor')), may hold values from -6 to 6
- gate_weight: bfloat16 [2, 3072, 9216], P(None, 'dp', 'tensor'), may hold values from -0.15625 to 0.15625
- up_weight: bfloat16 [2, 3072, 9216], P(None, 'dp', 'tensor'), may hold values from -0.15625 to 0.15625
- keep_mask: int32 [2, 2, 48, 144], replicated, may hold values from 0 to 1, as said below
Outputs:
- hidden: bfloat16 [2, 2048, 9216], P(None, 'dp', 'tensor')
Inputs may be any that keep to these rules, and one draw needn't show every extreme that they name: `keep_mask`: within each device's share of a projection (6 x 36 blocks: block rows of one dp index, block columns of one tensor index) at least one and at most 108 blocks are kept, and for each direction and projection some share keeps exactly 108.
All inputs are finite; a program needn't handle non-finite values.
Results may differ from a plain program's by a relative error of at most 0.001.
Values may be sent and summed in bfloat16 or wider, within the bound.
No kernel may reach another device: no remote copies, remote signals or barrier semaphores. Data moves between devices by JAX's collectives and lax.ppermute only.
A program may use at most 192 MiB of HBM per device.

v0:
```python
import jax
import jax.numpy as jnp
from jax import lax
from jax.sharding import PartitionSpec as P

BLOCK = 64


def expand_blocks(block_mask, block_width):
    return jnp.repeat(jnp.repeat(block_mask, block_width, axis=-2), block_width, axis=-1)


def shards(source_rows, gate_weight, up_weight, keep_mask):
    token_slab = lax.all_gather(source_rows, "tensor", axis=1, tiled=True)
    row_blocks = gate_weight.shape[1] // BLOCK
    col_blocks = gate_weight.shape[2] // BLOCK
    dp_index = lax.axis_index("dp")
    tensor_index = lax.axis_index("tensor")
    mask_cols = lax.dynamic_slice_in_dim(keep_mask, tensor_index * col_blocks, col_blocks, 3)
    own_mask = lax.dynamic_slice_in_dim(mask_cols, dp_index * row_blocks, row_blocks, 2)
    stacked = jnp.stack([gate_weight, up_weight], axis=1)
    kept_rows = stacked * expand_blocks(own_mask, BLOCK).astype(jnp.bfloat16)
    weights = lax.all_gather(kept_rows, "dp", axis=2, tiled=True)
    gate_sum = jnp.einsum(
        "mgd,mdf->mgf", token_slab, weights[:, 0], preferred_element_type=jnp.float32
    )
    up_sum = jnp.einsum(
        "mgd,mdf->mgf", token_slab, weights[:, 1], preferred_element_type=jnp.float32
    )
    return (jax.nn.silu(gate_sum) * up_sum).astype(jnp.bfloat16)


def solution(mesh):
    placed = (
        P(None, ("dp", "tensor"), None),
        P(None, "dp", "tensor"),
        P(None, "dp", "tensor"),
        P(),
    )
    return jax.shard_map(
        shards, mesh=mesh, in_specs=placed, out_specs=P(None, "dp", "tensor"), check_vma=False
    )
```

profile of v0, /device:TPU:0, one launch (start us, length us, event | category | flops | bytes accessed | tf_op | source)
XLA Modules:
  0.0 1152.1 jit_solution(3198824043148178128)
XLA Ops:
  6.5 0.0 all-gather.5.cloned.1.call-start
  6.5 0.7 all-gather.5.cloned.1.call-update
  7.3 0.0 all-gather.3.cloned.1.call-start
  7.3 0.9 dynamic-slice_convert_fusion
  8.2 0.1 copy.11
  8.4 0.2 broadcast_in_dim.6
  8.6 0.2 convert_element_type.15
  8.8 0.7 copy.12
  9.5 4.6 copy.9
  14.1 5.8 copy.10
  20.0 5.9 maximum_multiply_fusion
  25.9 0.0 all-gather.3.cloned.1.call-update
  26.0 14.2 %all-gather.5.cloned.1.call-done = bf16[2,256,3072]{2,1,0:T(8,128)(2,1)} async-done(((bf16[2,64,3072]{2,1,0:T(8,128)(2,1)}), bf16[2,256,3072]{2,1,0:T(8,128)(2,1)}) %all-gather.5.cloned.1.call-update) | async-done | bytes 3145744 | tf_op jit(solution)/shard_map/all_gather | solution.py:14
  40.2 1071.8 %all-gather.3.cloned.1.call-done = bf16[2,2,3072,2304]{2,3,0,1:T(8,128)(2,1)} async-done(((bf16[2,2,384,2304]{2,3,0,1:T(8,128)(2,1)}), bf16[2,2,3072,2304]{2,3,0,1:T(8,128)(2,1)}) %all-gather.3.cloned.1.call-update) | async-done | bytes 56623120 | tf_op jit(solution)/shard_map/all_gather | solution.py:23
  1112.0 15.3 %fusion.2 = f32[2,256,2304]{1,2,0:T(8,128)} fusion(bf16[2,256,3072]{2,1,0:T(8,128)(2,1)} %all-gather.5.cloned.1.call-done, bf16[2,2,3072,2304]{2,3,0,1:T(8,128)(2,1)} %all-gather.3.cloned.1.call-done), kind=kOutput, calls=%fused_computation.5 | convolution fusion | flops 7247757312 | bytes 36175872 | tf_op jit(solution)/shard_map/mgd,mdf->mgf/dot_general | solution.py:24
  1127.2 15.6 %fusion.5 = bf16[2,256,2304]{1,2,0:T(8,128)(2,1)S(1)} fusion(bf16[2,256,3072]{2,1,0:T(8,128)(2,1)} %all-gather.5.cloned.1.call-done, bf16[2,2,3072,2304]{2,3,0,1:T(8,128)(2,1)} %all-gather.3.cloned.1.call-done, f32[2,256,2304]{1,2,0:T(8,128)} %fusion.2), kind=kOutput, calls=%fused_computation.8 | convolution fusion | flops 7254835200 | bytes 38535168 | tf_op jit(solution)/shard_map/mgd,mdf->mgf/dot_general | solution.py:27
  1142.9 2.4 copy.13
Async XLA Ops:
  6.5 33.6 %all-gather.5.cloned.1.call-start = ((), (), s32[]{:S(2)}) async-start(), calls=%async_computation.1 | async-start | bytes 3932160 | tf_op jit(solution)/shard_map/all_gather | solution.py:14
  7.3 1104.7 %all-gather.3.cloned.1.call-start = ((), (), s32[]{:S(2)}) async-start(), calls=%async_computation | async-start | bytes 63700992 | tf_op jit(solution)/shard_map/all_gather | solution.py:23
Sparse Core Ops, SparseCore 0:
  8.9 31.2 all-gather.4
  41.7 1070.2 all-gather.2
where the time goes:
time: 1150 us
  waiting for transfers between devices  1090 us (95%)
  matrix products  30.9 us (3%)
  local copies, waits for them, and re-layouts  14.2 us (1%)
  between operations  13.4 us (1%)
    all_gather x1, waiting for transfers between devices, shards(): weights = lax.all_gather(kept_rows, 'dp', axis=2, tiled=True)  1070 us
  transfers between devices with their start and end apart: 2, of which 2 were waited for; matrix products, arithmetic and copies ran while one was open for 2% of the time, Pallas kernels for 0%

commit v1 on v0

--- a/solution.py
+++ b/solution.py
@@ -4,6 +4,12 @@
 from jax.sharding import PartitionSpec as P
 
 BLOCK = 64
+
+
+def laid_out(blocks, dim):
+    shape = list(blocks.shape[1:])
+    shape[dim] *= blocks.shape[0]
+    return jnp.moveaxis(blocks, 0, dim).reshape(shape)
 
 
 def expand_blocks(block_mask, block_width):
@@ -20,7 +26,19 @@
     own_mask = lax.dynamic_slice_in_dim(mask_cols, dp_index * row_blocks, row_blocks, 2)
     stacked = jnp.stack([gate_weight, up_weight], axis=1)
     kept_rows = stacked * expand_blocks(own_mask, BLOCK).astype(jnp.bfloat16)
-    weights = lax.all_gather(kept_rows, "dp", axis=2, tiled=True)
+    devices = lax.axis_size("dp")
+    pairs = [(i, (i + 1) % devices) for i in range(devices)]
+    back = [(b, a) for a, b in pairs]
+    lower, upper = ([], [])
+    for step in range(devices - 1):
+        if step % 2 == 0:
+            lower.append(lax.ppermute(lower[-1] if lower else kept_rows, "dp", pairs))
+        else:
+            upper.append(lax.ppermute(upper[-1] if upper else kept_rows, "dp", back))
+    tiles = jnp.stack([*lower[::-1], kept_rows, *upper])
+    shift = lax.axis_index("dp") - len(lower)
+    tiles = tiles[(jnp.arange(devices) - shift) % devices]
+    weights = laid_out(tiles, 2)
     gate_sum = jnp.einsum(
         "mgd,mdf->mgf", token_slab, weights[:, 0], preferred_element_type=jnp.float32
     )

time: 1150 us -> 1460 us (1.27)
  local copies, waits for them, and re-layouts: 14.2 us -> 294 us
  other arithmetic: 6.88 us -> 49.4 us
  waiting for transfers between devices: 1090 us -> 1050 us
  starting transfers between devices: 0.04 us -> 17.2 us
    all_gather x1 -> x0, waiting for transfers between devices: 1070 us -> none  [shards(): weights = lax.all_gather(kept_rows, 'dp', axis=2, tiled=True)]
    ppermute x0 -> x7, waiting for transfers between devices: none -> 1050 us  [the longest x4 1050 us: shards(): lower.append(lax.ppermute(lower[-1] if lower else kept_rows, 'dp', pairs))]
    gather x0 -> x6, local copies, waits for them, and re-layouts: none -> 87.7 us  [shards(): tiles = tiles[(jnp.arange(devices) - shift) % devices]]
    reshape x0 -> x1, local copies, waits for them, and re-layouts: none -> 82.8 us  [laid_out(): return jnp.moveaxis(blocks, 0, dim).reshape(shape)]
    transpose x0 -> x1, local copies, waits for them, and re-layouts: none -> 56.9 us  [laid_out(): return jnp.moveaxis(blocks, 0, dim).reshape(shape)]
    unnamed x2 -> x18, local copies, waits for them, and re-layouts: 10.5 us -> 53.1 us
    transpose x0 -> x1, other arithmetic: none -> 36.7 us  [laid_out(): return jnp.moveaxis(blocks, 0, dim).reshape(shape)]
    ppermute x0 -> x7, starting transfers between devices: none -> 17.2 us  [the longest x3 9.15 us: shards(): upper.append(lax.ppermute(upper[-1] if upper else kept_rows, 'dp', back))]
  transfers between devices with their start and end apart: 2 -> 8, of which waited for: 2 -> 4; matrix products, arithmetic and copies ran while one was open for 2% -> 22% of each run, Pallas kernels for 0% -> 0%
where the time goes in v1:
time: 1460 us
  waiting for transfers between devices  1050 us (72%)
  local copies, waits for them, and re-layouts  294 us (20%)
  other arithmetic  49.4 us (3%)
  matrix products  31 us (2%)
  starting transfers between devices  17.2 us (1%)
    ppermute x4, waiting for transfers between devices, shards(): lower.append(lax.ppermute(lower[-1] if lower else kept_rows, 'dp', pairs))  1050 us
    gather x6, local copies, waits for them, and re-layouts, shards(): tiles = tiles[(jnp.arange(devices) - shift) % devices]  87.7 us
    reshape x1, local copies, waits for them, and re-layouts, laid_out(): return jnp.moveaxis(blocks, 0, dim).reshape(shape)  82.8 us
    transpose x1, local copies, waits for them, and re-layouts, laid_out(): return jnp.moveaxis(blocks, 0, dim).reshape(shape)  56.9 us
    unnamed x18, local copies, waits for them, and re-layouts  53.1 us
    transpose x1, other arithmetic, laid_out(): return jnp.moveaxis(blocks, 0, dim).reshape(shape)  36.7 us
  transfers between devices with their start and end apart: 8, of which 4 were waited for; matrix products, arithmetic and copies ran while one was open for 22% of the time, Pallas kernels for 0%

profile of v1, /device:TPU:0, one launch (start us, length us, event | category | flops | bytes accessed | tf_op | source)
XLA Modules:
  0.0 1459.4 jit_solution(14919670824037867814)
XLA Ops:
  6.5 0.0 all-gather.2.cloned.1.call-start
  6.5 0.9 dynamic-slice_convert_fusion
  7.5 0.1 copy.17
  7.6 0.2 broadcast_in_dim.7
  7.8 0.2 convert_element_type.28
  8.0 0.7 copy.18
  8.7 4.6 copy.15
  13.3 5.8 copy.16
  19.1 3.0 maximum_multiply_fusion
  22.1 3.0 collective-permute-start
  25.1 155.3 %collective-permute-done = bf16[2,2,384,2304]{2,3,1,0:T(8,128)(2,1)S(1)} collective-permute-done((bf16[2,2,384,2304]{2,3,1,0:T(8,128)(2,1)S(1)}, bf16[2,2,384,2304]{2,3,1,0:T(8,128)(2,1)S(1)}, u32[]{:S(2)}, u32[]{:S(2)}) %collective-permute-start) | collective-permute-done | bytes 7077920 | tf_op jit(solution)/shard_map/ppermute | solution.py:35
  180.4 3.0 copy-done
  183.4 0.0 collective-permute-start.1
  183.4 4.7 collective-permute-start.4
  188.1 298.3 %collective-permute-done.1 = bf16[2,2,384,2304]{2,3,1,0:T(8,128)(2,1)S(1)} collective-permute-done((bf16[2,2,384,2304]{2,3,1,0:T(8,128)(2,1)S(1)}, bf16[2,2,384,2304]{2,3,1,0:T(8,128)(2,1)S(1)}, u32[]{:S(2)}, u32[]{:S(2)}) %collective-permute-start.1) | collective-permute-done | bytes 7077920 | tf_op jit(solution)/shard_map/ppermute | solution.py:35
  486.4 2.8 copy-done.1
  489.2 2.5 collective-permute-start.2
  491.7 0.0 collective-permute-done.4
  491.7 2.2 collective-permute-start.5
  493.9 299.9 %collective-permute-done.2 = bf16[2,2,384,2304]{2,3,1,0:T(8,128)(2,1)} collective-permute-done((bf16[2,2,384,2304]{2,3,1,0:T(8,128)(2,1)S(1)}, bf16[2,2,384,2304]{2,3,1,0:T(8,128)(2,1)}, u32[]{:S(2)}, u32[]{:S(2)}) %collective-permute-start.2) | collective-permute-done | bytes 7077920 | tf_op jit(solution)/shard_map/ppermute | solution.py:35
  793.9 2.6 collective-permute-start.3
  796.5 0.0 all-gather.2.cloned.1.call-update
  796.5 0.0 collective-permute-done.5
  796.5 2.2 collective-permute-start.6
  798.7 300.4 %collective-permute-done.3 = bf16[2,2,384,2304]{2,3,1,0:T(8,128)(2,1)} collective-permute-done((bf16[2,2,384,2304]{2,3,1,0:T(8,128)(2,1)}, bf16[2,2,384,2304]{2,3,1,0:T(8,128)(2,1)}, u32[]{:S(2)}, u32[]{:S(2)}) %collective-permute-start.3) | collective-permute-done | bytes 7077920 | tf_op jit(solution)/shard_map/ppermute | solution.py:35
  1099.2 6.6 bitcast_dynamic-update-slice_fusion.6
  1105.8 6.8 bitcast_dynamic-update-slice_fusion.5
  1112.6 6.7 bitcast_dynamic-update-slice_fusion.4
  1119.3 0.0 slice-done.1
  1119.3 3.6 bitcast_dynamic-update-slice_fusion.3
  1122.9 3.6 broadcast_in_dim.8
  1126.5 8.8 fusion.2
  1135.3 6.6 bitcast_dynamic-update-slice_fusion.2
  1141.9 6.6 bitcast_dynamic-update-slice_fusion.1
  1148.4 0.0 collective-permute-done.6
  1148.4 6.6 bitcast_dynamic-update-slice_fusion
  1155.0 31.2 %fusion.9 = (bf16[8,2,2,384,640]{3,4,2,1,0:T(8,128)(2,1)}, bf16[8,2,2,384,640]{3,4,2,1,0:T(8,128)(2,1)}, bf16[8,2,2,384,640]{3,4,2,1,0:T(8,128)(2,1)}) fusion(bf16[8,2,2,384,2304]{3,4,2,1,0:T(8,128)(2,1)} %bitcast_dynamic-update-slice_fusion), kind=kLoop, calls=%fused_computation.31 | loop fusion | bytes 94371840 | tf_op jit(solution)/shard_map/gather | solution.py:40
  1186.2 8.8 mini-gather-slice.7
  1195.0 12.8 gather_fusion
  1207.8 12.8 gather_fusion.1
  1220.6 12.8 gather_fusion.2
  1233.4 9.3 gather_fusion.3
  1242.7 36.7 %maximum_bitcast_fusion = bf16[2,2,8,384,2304]{3,4,1,0,2:T(8,128)(2,1)} fusion(bf16[8,2,2,384,384]{3,4,2,1,0:T(8,128)(2,1)} %gather_fusion.3, bf16[8,2,2,384,640]{3,4,2,1,0:T(8,128)(2,1)} %gather_fusion.2, bf16[8,2,2,384,640]{3,4,2,1,0:T(8,128)(2,1)} %gather_fusion.1, bf16[8,2,2,384,640]{3,4,2,1,0:T(8,128)(2,1)} %gather_fusion), kind=kLoop, calls=%fused_computation.4 | loop fusion | flops 226492416 | bytes 113246208 | tf_op jit(solution)/shard_map/transpose | solution.py:12
  1279.4 56.9 %copy.21 = bf16[2,2,8,384,2304]{3,2,4,0,1:T(8,128)(2,1)} copy(bf16[2,2,8,384,2304]{3,4,1,0,2:T(8,128)(2,1)} %maximum_bitcast_fusion) | data formatting | bytes 113246208 | tf_op jit(solution)/shard_map/transpose | solution.py:12
  1336.3 82.8 %reshape.99 = bf16[2,2,3072,2304]{2,3,0,1:T(8,128)(2,1)} reshape(bf16[2,2,8,384,2304]{3,2,4,0,1:T(8,128)(2,1)} %copy.21) | data formatting | bytes 113246208 | tf_op jit(solution)/shard_map/reshape | solution.py:12
  1419.1 15.3 %fusion.3 = f32[2,256,2304]{1,2,0:T(8,128)} fusion(bf16[2,256,3072]{2,1,0:T(8,128)(2,1)} %all-gather.2.cloned.1.call-done, bf16[2,2,3072,2304]{2,3,0,1:T(8,128)(2,1)} %reshape.99), kind=kOutput, calls=%fused_computation.19 | convolution fusion | flops 7247757312 | bytes 36175872 | tf_op jit(solution)/shard_map/mgd,mdf->mgf/dot_general | solution.py:42
  1434.4 15.7 %fusion.6 = bf16[2,256,2304]{1,2,0:T(8,128)(2,1)S(1)} fusion(bf16[2,256,3072]{2,1,0:T(8,128)(2,1)} %all-gather.2.cloned.1.call-done, bf16[2,2,3072,2304]{2,3,0,1:T(8,128)(2,1)} %reshape.99, f32[2,256,2304]{1,2,0:T(8,128)} %fusion.3), kind=kOutput, calls=%fused_computation.22 | convolution fusion | flops 7254835200 | bytes 38535168 | tf_op jit(solution)/shard_map/mgd,mdf->mgf/dot_general | solution.py:45
  1450.1 2.4 copy.22
  (11 shorter events, 0.0 us)
Async XLA Ops:
  6.5 1412.5 %all-gather.2.cloned.1.call-start = ((), (), s32[]{:S(2)}) async-start(), calls=%async_computation | async-start | bytes 3932160 | tf_op jit(solution)/shard_map/all_gather | solution.py:20
  22.1 158.3 %collective-permute-start = (bf16[2,2,384,2304]{2,3,1,0:T(8,128)(2,1)S(1)}, bf16[2,2,384,2304]{2,3,1,0:T(8,128)(2,1)S(1)}, u32[]{:S(2)}, u32[]{:S(2)}) collective-permute-start(bf16[2,2,384,2304]{2,3,1,0:T(8,128)(2,1)S(1)} %maximum_multiply_fusion), channel_id=1, source_target_pairs={{0,4},{4,8},{8,12},{12,16},{16,20},{20,24},{24,28},{28,0},{1,5},{5... | collective-permute-start | bytes 21233672 | tf_op jit(solution)/shard_map/ppermute | solution.py:35
  180.4 3.0 copy-start
  183.4 303.0 %collective-permute-start.1 = (bf16[2,2,384,2304]{2,3,1,0:T(8,128)(2,1)S(1)}, bf16[2,2,384,2304]{2,3,1,0:T(8,128)(2,1)S(1)}, u32[]{:S(2)}, u32[]{:S(2)}) collective-permute-start(bf16[2,2,384,2304]{2,3,1,0:T(8,128)(2,1)S(1)} %collective-permute-done), channel_id=1, source_target_pairs={{0,4},{4,8},{8,12},{12,16},{16,20},{20,24},{24,28},{28,0},{1,5},{5... | collective-permute-start | bytes 21233672 | tf_op jit(solution)/shard_map/ppermute | solution.py:35
  183.4 308.3 %collective-permute-start.4 = (bf16[2,2,384,2304]{2,3,1,0:T(8,128)(2,1)S(1)}, bf16[2,2,384,2304]{2,3,1,0:T(8,128)(2,1)}, u32[]{:S(2)}, u32[]{:S(2)}) collective-permute-start(bf16[2,2,384,2304]{2,3,1,0:T(8,128)(2,1)S(1)} %maximum_multiply_fusion), channel_id=1, source_target_pairs={{4,0},{8,4},{12,8},{16,12},{20,16},{24,20},{28,24},{0,28},{5,1},{9... | collective-permute-start | bytes 21233672 | tf_op jit(solution)/shard_map/ppermute | solution.py:37
  486.4 2.8 copy-start.1
  489.2 304.7 %collective-permute-start.2 = (bf16[2,2,384,2304]{2,3,1,0:T(8,128)(2,1)S(1)}, bf16[2,2,384,2304]{2,3,1,0:T(8,128)(2,1)}, u32[]{:S(2)}, u32[]{:S(2)}) collective-permute-start(bf16[2,2,384,2304]{2,3,1,0:T(8,128)(2,1)S(1)} %collective-permute-done.1), channel_id=1, source_target_pairs={{0,4},{4,8},{8,12},{12,16},{16,20},{20,24},{24,28},{28,0},{1,5},{5... | collective-permute-start | bytes 21233672 | tf_op jit(solution)/shard_map/ppermute | solution.py:35
  491.7 304.8 %collective-permute-start.5 = (bf16[2,2,384,2304]{2,3,1,0:T(8,128)(2,1)}, bf16[2,2,384,2304]{2,3,1,0:T(8,128)(2,1)}, u32[]{:S(2)}, u32[]{:S(2)}) collective-permute-start(bf16[2,2,384,2304]{2,3,1,0:T(8,128)(2,1)} %collective-permute-done.4), channel_id=1, source_target_pairs={{4,0},{8,4},{12,8},{16,12},{20,16},{24,20},{28,24},{0,28},{5,1},{9... | collective-permute-start | bytes 21233672 | tf_op jit(solution)/shard_map/ppermute | solution.py:37
  793.9 305.3 %collective-permute-start.3 = (bf16[2,2,384,2304]{2,3,1,0:T(8,128)(2,1)}, bf16[2,2,384,2304]{2,3,1,0:T(8,128)(2,1)}, u32[]{:S(2)}, u32[]{:S(2)}) collective-permute-start(bf16[2,2,384,2304]{2,3,1,0:T(8,128)(2,1)} %collective-permute-done.2), channel_id=1, source_target_pairs={{0,4},{4,8},{8,12},{12,16},{16,20},{20,24},{24,28},{28,0},{1,5},{5... | collective-permute-start | bytes 21233672 | tf_op jit(solution)/shard_map/ppermute | solution.py:35
  796.5 351.9 %collective-permute-start.6 = (bf16[2,2,384,2304]{2,3,1,0:T(8,128)(2,1)}, bf16[2,2,384,2304]{2,3,1,0:T(8,128)(2,1)}, u32[]{:S(2)}, u32[]{:S(2)}) collective-permute-start(bf16[2,2,384,2304]{2,3,1,0:T(8,128)(2,1)} %collective-permute-done.5), channel_id=1, source_target_pairs={{4,0},{8,4},{12,8},{16,12},{20,16},{24,20},{28,24},{0,28},{5,1},{9... | collective-permute-start | bytes 21233672 | tf_op jit(solution)/shard_map/ppermute | solution.py:37
  1105.8 13.5 slice-start
  1112.6 6.7 slice-start.1
  1112.6 10.3 copy-start.2
Sparse Core Ops, SparseCore 0:
  796.6 26.8 all-gather.1
